TPU v7x, 256 devices: a whole 4x4x8 slice. The times are simulated.
256 devices in a mesh: section: 2 (over core), seq: 16 (over x, y), tensor: 8 (over z).
Axes of the slice: x: 4, y: 4, z: 8, core: 2. Of those that a mesh axis runs over, the one named last changes fastest.
Arguments:
- x_in: bfloat16 [2, 32768, 2048], P(None, 'seq', 'tensor'), may hold values from -6 to 6
- norm_gain: float32 [2, 2048], P('section', 'tensor'), may hold values from 0.5 to 1.5
- right_blocks: bfloat16 [2, 128, 256, 256], P('section', 'seq'), may hold values from -0.375 to 0.375
- left_blocks: bfloat16 [2, 256, 128, 128], P('section', 'seq'), may hold values from -0.5 to 0.5
- gate_first: bfloat16 [2, 32, 64, 64], P('section'), may hold values from -0.75 to 0.75
- gate_second: bfloat16 [2, 64, 32, 32], P('section'), may hold values from -1 to 1
- out_first: bfloat16 [2, 32, 64, 64], P('section'), may hold values from -0.75 to 0.75
- out_second: bfloat16 [2, 64, 32, 32], P('section'), may hold values from -1 to 1
- head: bfloat16 [2, 2048, 32768], P('section', None, ('seq', 'tensor')), may hold values from -0.375 to 0.375
- targets: int32 [2, 256], replicated, may hold values from 0 to 32767
Outputs:
- block_out: bfloat16 [2, 2, 32768, 2048], P('section', None, 'seq', 'tensor')
- aux_losses: float32 [2, 2, 256], P('section')
All inputs are finite; a program needn't handle non-finite values.
Results may differ from a plain program's by a relative error of at most 0.011.
Values may be sent and summed in bfloat16 or wider, within the bound.
No kernel may reach another device: no remote copies, remote signals or barrier semaphores. Data moves between devices by JAX's collectives and lax.ppermute only.
A program may use at most 128 MiB of HBM per device.

v0:
```python
import jax
import jax.numpy as jnp
from jax import lax
from jax.sharding import PartitionSpec as P

C1 = 32
C2 = 64
D = 2048
STRIDE = 128
epsilon = 1e-05


def from_behind(block, axis, distance):
    devices = range(lax.axis_size(axis))
    route = [(i - distance, i) for i in devices if i - distance in devices]
    return lax.ppermute(block, axis, route)


def first_map(factor_local):
    c_one, c_two, _ = factor_local.shape
    identity = jnp.eye(c_one, dtype=factor_local.dtype)
    dense_map = identity[None, :, :, None] * jnp.transpose(factor_local, (1, 0, 2))[:, :, None, :]
    return dense_map.reshape(c_two * c_one, c_one * c_two)


def second_map(factor_local, groups, c_one):
    k_dev = factor_local.shape[0]
    split_view = factor_local.reshape(k_dev, groups, c_one, groups, c_one)
    split_view = jnp.transpose(split_view, (1, 2, 0, 3, 4))
    identity = jnp.eye(k_dev, dtype=factor_local.dtype)
    dense_map = split_view[:, :, :, :, None, :] * identity[None, None, :, None, :, None]
    return dense_map.reshape(groups * c_one * k_dev, groups * k_dev * c_one)


def restore_rows(returned, groups, c_one, k_dev, token_count):
    ordered = returned.reshape(groups, c_one, k_dev, token_count)
    return jnp.transpose(ordered, (3, 1, 0, 2)).reshape(token_count, c_one * groups * k_dev)


def gate_channels(normed, one_map, two_map, groups, c_one, k_dev):
    token_count = normed.shape[0]
    first_mix = jnp.einsum("oc,tc->ot", one_map, normed, preferred_element_type=jnp.float32).astype(
        jnp.bfloat16
    )
    first_mix = first_mix.reshape(groups, k_dev * c_one, token_count)
    incoming = lax.all_to_all(first_mix, "tensor", split_axis=0, concat_axis=0, tiled=True)
    count_here = incoming.shape[2]
    flat_in = incoming.reshape(groups * k_dev * c_one, count_here)
    second_mix = jnp.dot(two_map, flat_in, preferred_element_type=jnp.float32).astype(jnp.bfloat16)
    returned = lax.all_to_all(
        second_mix.reshape(groups, c_one * k_dev, count_here),
        "tensor",
        split_axis=0,
        concat_axis=0,
        tiled=True,
    )
    return restore_rows(returned, groups, c_one, k_dev, token_count)


def out_channels(values, one_map, two_map, groups, c_one, k_dev):
    token_count = values.shape[0]
    first_mix = jnp.einsum("oc,tc->ot", one_map, values, preferred_element_type=jnp.float32).astype(
        jnp.bfloat16
    )
    first_mix = first_mix.reshape(groups, k_dev * c_one, token_count)
    incoming = lax.all_to_all(first_mix, "tensor", split_axis=0, concat_axis=0, tiled=True)
    count_here = incoming.shape[2]
    flat_in = incoming.reshape(groups * k_dev * c_one, count_here)
    second_mix = jnp.dot(two_map, flat_in, preferred_element_type=jnp.float32).astype(jnp.bfloat16)
    returned = lax.all_to_all(
        second_mix.reshape(groups, c_one * k_dev, count_here),
        "tensor",
        split_axis=0,
        concat_axis=0,
        tiled=True,
    )
    return restore_rows(returned, groups, c_one, k_dev, token_count)


def sequence_mix(normed, right_local, left_local, row_count, col_count):
    chan_count = normed.shape[1]
    seq_view = normed.reshape(row_count, col_count, chan_count)
    row_mix = jnp.einsum(
        "pjq,pqc->pjc", right_local, seq_view, preferred_element_type=jnp.float32
    ).astype(jnp.bfloat16)
    col_mix = jnp.einsum(
        "jip,pjc->ijc",
        left_local,
        lax.all_to_all(row_mix, "seq", split_axis=1, concat_axis=0, tiled=True),
        preferred_element_type=jnp.float32,
    ).astype(jnp.bfloat16)
    returned = lax.all_to_all(col_mix, "seq", split_axis=0, concat_axis=1, tiled=True)
    return returned.reshape(row_count * col_count, chan_count)


def body(
    x_in,
    norm_gain,
    right_blocks,
    left_blocks,
    gate_first,
    gate_second,
    out_first,
    out_second,
    head,
    targets,
):
    section_index = lax.axis_index("section")
    tensor_count = lax.axis_size("tensor")
    tensor_index = lax.axis_index("tensor")
    micro_count = x_in.shape[0]
    tok_dev = x_in.shape[1]
    chan_dev = x_in.shape[2]
    row_count = right_blocks.shape[1]
    col_count = right_blocks.shape[2]
    c_one = C1 // tensor_count
    k_dev = C2 // tensor_count
    norm_scale = norm_gain[0]
    right_local = right_blocks[0]
    left_local = left_blocks[0]
    gate_first_all = gate_first[0]
    gate_second_all = gate_second[0]
    out_first_all = out_first[0]
    out_second_all = out_second[0]
    gate_one = first_map(lax.dynamic_slice_in_dim(gate_first_all, tensor_index * c_one, c_one, 0))
    gate_two = second_map(
        lax.dynamic_slice_in_dim(gate_second_all, tensor_index * k_dev, k_dev, 0),
        tensor_count,
        c_one,
    )
    out_one = first_map(lax.dynamic_slice_in_dim(out_first_all, tensor_index * c_one, c_one, 0))
    out_two = second_map(
        lax.dynamic_slice_in_dim(out_second_all, tensor_index * k_dev, k_dev, 0),
        tensor_count,
        c_one,
    )
    head_local = head[0]
    vocab_dev = head_local.shape[1]
    vocab_offset = lax.axis_index(("seq", "tensor")) * vocab_dev
    handed = jnp.zeros((tok_dev, chan_dev), jnp.bfloat16)
    first_outputs, second_outputs, first_losses, second_losses = ([], [], [], [])
    for step_index in range(micro_count + 1):
        feed_rows = x_in[min(step_index, micro_count - 1)]
        x_val = jnp.where(section_index == 0, feed_rows, handed)
        labels = jnp.where(
            section_index == 0,
            targets[min(step_index, micro_count - 1)],
            targets[max(step_index - 1, 0)],
        )
        x_float = x_val.astype(jnp.float32)
        square_part = jnp.sum(x_float * x_float, axis=1)
        square_total = lax.psum(square_part, "tensor")
        row_scale = lax.rsqrt(square_total / D + epsilon)
        normed = (x_float * row_scale[:, None] * norm_scale[None, :]).astype(jnp.bfloat16)
        seq_out = sequence_mix(normed, right_local, left_local, row_count, col_count)
        gate_pre = gate_channels(normed, gate_one, gate_two, tensor_count, c_one, k_dev)
        gated_mix = (
            seq_out.astype(jnp.float32) * jax.nn.sigmoid(gate_pre.astype(jnp.float32))
        ).astype(jnp.bfloat16)
        out_pre = out_channels(gated_mix, out_one, out_two, tensor_count, c_one, k_dev)
        result = (x_float + out_pre.astype(jnp.float32)).astype(jnp.bfloat16)
        scored = result.reshape(row_count, col_count, chan_dev)[:, ::STRIDE, :].reshape(
            -1, chan_dev
        )
        wide_rows = lax.all_gather(scored, "tensor", axis=1, tiled=True)
        logits = jnp.dot(
            lax.all_gather(wide_rows, "seq", axis=0, tiled=True),
            head_local,
            preferred_element_type=jnp.float32,
        )
        exp_sums = jnp.sum(jnp.exp(logits), axis=1)
        vocab_ids = jnp.arange(vocab_dev, dtype=jnp.int32)[None, :] + vocab_offset
        is_target = vocab_ids == labels[:, None]
        target_part = jnp.sum(jnp.where(is_target, logits, 0.0), axis=1)
        exp_total, target_logit = lax.psum((exp_sums, target_part), ("seq", "tensor"))
        result, aux_loss = (result, jnp.log(exp_total) - target_logit)
        if step_index < micro_count:
            first_outputs.append(result)
            first_losses.append(aux_loss)
            handed = from_behind(result, "section", 1)
        if step_index > 0:
            second_outputs.append(result)
            second_losses.append(aux_loss)
    block_out = jnp.where(section_index == 0, jnp.stack(first_outputs), jnp.stack(second_outputs))[
        None
    ]
    aux_losses = jnp.where(section_index == 0, jnp.stack(first_losses), jnp.stack(second_losses))[
        None
    ]
    return (block_out, aux_losses)


def solution(mesh):
    in_specs = (
        P(None, "seq", "tensor"),
        P("section", "tensor"),
        P("section", "seq", None, None),
        P("section", "seq", None, None),
        P("section", None, None, None),
        P("section", None, None, None),
        P("section", None, None, None),
        P("section", None, None, None),
        P("section", None, ("seq", "tensor")),
        P(),
    )
    out_specs = (P("section", None, "seq", "tensor"), P("section", None, None))
    return jax.shard_map(body, mesh=mesh, in_specs=in_specs, out_specs=out_specs, check_vma=False)
```

profile of v0, /device:TPU:0, one launch (start us, length us, event | category | flops | bytes accessed | tf_op | source)
XLA Modules:
  0.0 1093.3 jit_solution(17827740526057056564)
XLA Ops:
  13.2 18.5 %psum.63 = f32[2048]{0:T(1024)S(1)} all-reduce(f32[2048]{0:T(1024)S(1)} %fusion.18), channel_id=1, replica_groups=mesh['section'=2,'seq'=16,'tensor'=8] {'tensor'}, use_global_device_ids=true, to_apply=%region_1.2 | all-reduce | flops 2048 | bytes 16384 | tf_op jit(solution)/shard_map/psum | solution.py:152
  43.1 19.9 %all-to-all-done.2 = bf16[8,32,2048]{2,1,0:T(8,128)(2,1)} async-done(((bf16[8,32,2048]{2,1,0:T(8,128)(2,1)}), bf16[8,32,2048]{2,1,0:T(8,128)(2,1)}, u32[]{:S(2)}, u32[]{:S(2)}) %all-to-all-start.2) | async-done | bytes 1048608 | tf_op jit(solution)/shard_map/all_to_all | solution.py:46
  63.0 7.1 all-to-all-start
  93.4 17.9 %all-to-all-done.3 = bf16[8,32,2048]{2,1,0:T(8,128)(2,1)S(1)} async-done(((bf16[8,32,2048]{2,1,0:T(8,128)(2,1)}), bf16[8,32,2048]{2,1,0:T(8,128)(2,1)S(1)}, u32[]{:S(2)}, u32[]{:S(2)}) %all-to-all-start.3) | async-done | bytes 1048608 | tf_op jit(solution)/shard_map/all_to_all | solution.py:50
  117.2 9.1 reshape.474
  126.3 11.8 %copy.100 = f32[8,16,16,256]{3,2,0,1:T(8,128)S(1)} copy(f32[8,16,16,256]{2,1,0,3:T(8,128)} %reshape.474) | data formatting | bytes 4194304 | tf_op jit(solution)/shard_map/div | solution.py:158
  148.3 22.9 %all-to-all-done.4 = bf16[8,32,2048]{2,1,0:T(8,128)(2,1)} async-done(((bf16[8,32,2048]{2,1,0:T(8,128)(2,1)}), bf16[8,32,2048]{2,1,0:T(8,128)(2,1)}, u32[]{:S(2)}, u32[]{:S(2)}) %all-to-all-start.4) | async-done | bytes 1048608 | tf_op jit(solution)/shard_map/all_to_all | solution.py:66
  172.9 28.1 %all_to_all.141 = bf16[8,32,2048]{2,1,0:T(8,128)(2,1)S(1)} all-to-all(bf16[8,32,2048]{2,1,0:T(8,128)(2,1)S(1)} %bitcast.255), channel_id=1, replica_groups=mesh['section'=2,'seq'=16,'tensor'=8] {'tensor'}, dimensions={0} | all-to-all | bytes 2097152 | tf_op jit(solution)/shard_map/all_to_all | solution.py:70
  211.0 14.9 %psum.64 = f32[2048]{0:T(1024)S(1)} all-reduce(f32[2048]{0:T(1024)S(1)} %get-tuple-element.22), channel_id=1, replica_groups=mesh['section'=2,'seq'=16,'tensor'=8] {'tensor'}, use_global_device_ids=true, to_apply=%region_3.4 | all-reduce | flops 2048 | bytes 16384 | tf_op jit(solution)/shard_map/psum | solution.py:152
  239.5 20.1 %all-to-all-done.8 = bf16[8,32,2048]{2,1,0:T(8,128)(2,1)} async-done(((bf16[8,32,2048]{2,1,0:T(8,128)(2,1)}), bf16[8,32,2048]{2,1,0:T(8,128)(2,1)}, u32[]{:S(2)}, u32[]{:S(2)}) %all-to-all-start.8) | async-done | bytes 1048608 | tf_op jit(solution)/shard_map/all_to_all | solution.py:46
  259.6 7.0 all-to-all-start.6
  269.3 11.2 %all-to-all-done.6 = bf16[8,256,256]{2,0,1:T(8,128)(2,1)} async-done(((bf16[8,256,256]{2,0,1:T(8,128)(2,1)}), bf16[8,256,256]{2,0,1:T(8,128)(2,1)}, u32[]{:S(2)}, u32[]{:S(2)}) %all-to-all-start.6) | async-done | bytes 1048608 | tf_op jit(solution)/shard_map/all_to_all | solution.py:89
  290.5 17.9 %all-to-all-done.9 = bf16[8,32,2048]{2,1,0:T(8,128)(2,1)} async-done(((bf16[8,32,2048]{2,1,0:T(8,128)(2,1)}), bf16[8,32,2048]{2,1,0:T(8,128)(2,1)}, u32[]{:S(2)}, u32[]{:S(2)}) %all-to-all-start.9) | async-done | bytes 1048608 | tf_op jit(solution)/shard_map/all_to_all | solution.py:50
  316.3 10.4 reshape.479
  326.8 12.9 %copy.112 = f32[8,16,16,256]{3,2,0,1:T(8,128)} copy(f32[8,16,16,256]{2,1,0,3:T(8,128)} %reshape.479) | data formatting | bytes 4194304 | tf_op jit(solution)/shard_map/div | solution.py:158
  342.4 28.1 %all_to_all.142 = bf16[8,32,2048]{2,1,0:T(8,128)(2,1)S(1)} all-to-all(bf16[8,32,2048]{2,1,0:T(8,128)(2,1)S(1)} %bitcast.258), channel_id=1, replica_groups=mesh['section'=2,'seq'=16,'tensor'=8] {'tensor'}, dimensions={0} | all-to-all | bytes 2097152 | tf_op jit(solution)/shard_map/all_to_all | solution.py:66
  371.0 27.4 %all_to_all.143 = bf16[8,32,2048]{2,1,0:T(8,128)(2,1)S(1)} all-to-all(bf16[8,32,2048]{2,1,0:T(8,128)(2,1)S(1)} %bitcast.260), channel_id=1, replica_groups=mesh['section'=2,'seq'=16,'tensor'=8] {'tensor'}, dimensions={0} | all-to-all | bytes 2097152 | tf_op jit(solution)/shard_map/all_to_all | solution.py:70
  405.1 15.0 %psum.65 = f32[2048]{0:T(1024)S(1)} all-reduce(f32[2048]{0:T(1024)S(1)} %get-tuple-element.20), channel_id=1, replica_groups=mesh['section'=2,'seq'=16,'tensor'=8] {'tensor'}, use_global_device_ids=true, to_apply=%region_5.6 | all-reduce | flops 2048 | bytes 16384 | tf_op jit(solution)/shard_map/psum | solution.py:152
  433.7 20.5 %all-to-all-done.14 = bf16[8,32,2048]{2,1,0:T(8,128)(2,1)} async-done(((bf16[8,32,2048]{2,1,0:T(8,128)(2,1)}), bf16[8,32,2048]{2,1,0:T(8,128)(2,1)}, u32[]{:S(2)}, u32[]{:S(2)}) %all-to-all-start.14) | async-done | bytes 1048608 | tf_op jit(solution)/shard_map/all_to_all | solution.py:46
  454.1 6.9 all-to-all-start.12
  463.7 11.3 %all-to-all-done.12 = bf16[8,256,256]{2,0,1:T(8,128)(2,1)} async-done(((bf16[8,256,256]{2,0,1:T(8,128)(2,1)}), bf16[8,256,256]{2,0,1:T(8,128)(2,1)}, u32[]{:S(2)}, u32[]{:S(2)}) %all-to-all-start.12) | async-done | bytes 1048608 | tf_op jit(solution)/shard_map/all_to_all | solution.py:89
  484.9 18.1 %all-to-all-done.15 = bf16[8,32,2048]{2,1,0:T(8,128)(2,1)} async-done(((bf16[8,32,2048]{2,1,0:T(8,128)(2,1)}), bf16[8,32,2048]{2,1,0:T(8,128)(2,1)}, u32[]{:S(2)}, u32[]{:S(2)}) %all-to-all-start.15) | async-done | bytes 1048608 | tf_op jit(solution)/shard_map/all_to_all | solution.py:50
  511.0 10.4 reshape.483
  521.4 12.9 %copy.122 = f32[8,16,16,256]{3,2,0,1:T(8,128)} copy(f32[8,16,16,256]{2,1,0,3:T(8,128)} %reshape.483) | data formatting | bytes 4194304 | tf_op jit(solution)/shard_map/div | solution.py:158
  545.2 6.3 slice.28
  553.0 32.3 %all_gather.18 = bf16[16,2048]{1,0:T(8,128)(2,1)} all-gather(bf16[16,256]{1,0:T(8,128)(2,1)S(1)} %reshape.465), channel_id=1, replica_groups=mesh['section'=2,'seq'=16,'tensor'=8] {'tensor'}, dimensions={1}, use_global_device_ids=true | all-gather | bytes 73728 | tf_op jit(solution)/shard_map/all_gather | solution.py:165
  587.9 5.8 all-to-all-start.17
  597.3 35.3 %all_gather.20 = bf16[16,2048]{1,0:T(8,128)(2,1)} all-gather(bf16[16,256]{1,0:T(8,128)(2,1)S(1)} %reshape.467), channel_id=1, replica_groups=mesh['section'=2,'seq'=16,'tensor'=8] {'tensor'}, dimensions={1}, use_global_device_ids=true | all-gather | bytes 73728 | tf_op jit(solution)/shard_map/all_gather | solution.py:165
  640.3 26.5 %all_gather.22 = bf16[16,2048]{1,0:T(8,128)(2,1)} all-gather(bf16[16,256]{1,0:T(8,128)(2,1)S(1)} %reshape.469), channel_id=1, replica_groups=mesh['section'=2,'seq'=16,'tensor'=8] {'tensor'}, dimensions={1}, use_global_device_ids=true | all-gather | bytes 73728 | tf_op jit(solution)/shard_map/all_gather | solution.py:165
  671.7 11.2 %all-gather.6.cloned.1.call-done = bf16[256,2048]{1,0:T(8,128)(2,1)} async-done(((bf16[16,2048]{1,0:T(8,128)(2,1)}), bf16[256,2048]{1,0:T(8,128)(2,1)}) %all-gather.6.cloned.1.call-update) | async-done | bytes 1048592 | tf_op jit(solution)/shard_map/all_gather | solution.py:167
  691.5 40.9 %all-gather.8.cloned.1.call-done = bf16[256,2048]{1,0:T(8,128)(2,1)} async-done(((bf16[16,2048]{1,0:T(8,128)(2,1)}), bf16[256,2048]{1,0:T(8,128)(2,1)}) %all-gather.8.cloned.1.call-update) | async-done | bytes 1048592 | tf_op jit(solution)/shard_map/all_gather | solution.py:167
  734.2 351.8 %all-reduce = (f32[256]{0:T(256)S(1)}, f32[256]{0:T(256)S(1)}, f32[256]{0:T(256)S(1)}, f32[256]{0:T(256)S(1)}, f32[256]{0:T(256)S(1)}, /*index=5*/f32[256]{0:T(256)S(1)}) all-reduce(f32[256]{0:T(256)S(1)} %get-tuple-element.30, f32[256]{0:T(256)S(1)} %get-tuple-element.31, ...), channel_id=1, replica_groups=mesh['section'=2,'seq'=16,'tensor'=8] {'seq','tensor'}, use_global_device_ids=true, to_apply=%region_13.14 | all-reduce | flops 1536 | bytes 12288 | tf_op jit(solution)/shard_map/psum | solution.py:175
  (184 shorter events, 188.5 us)
Async XLA Ops:
  7.2 31.8 %copy-start = (bf16[1,8,256,256]{3,2,1,0:T(8,128)(2,1)S(1)}, bf16[1,8,256,256]{3,2,1,0:T(8,128)(2,1)}, u32[]{:S(2)}) copy-start(bf16[1,8,256,256]{3,2,1,0:T(8,128)(2,1)} %param.12) | copy-start | bytes 3145732
  9.5 22.2 %copy-start.19 = (bf16[256,256]{1,0:T(8,128)(2,1)}, bf16[256,256]{1,0:T(8,128)(2,1)S(1)}, u32[]{:S(2)}) copy-start(bf16[256,256]{1,0:T(8,128)(2,1)S(1)} %mul.236) | copy-start | bytes 393220
  12.3 19.5 %copy-start.26 = (f32[1,256]{1,0:T(1,128)S(1)}, f32[1,256]{1,0:T(1,128)}, u32[]{:S(2)}) copy-start(f32[1,256]{1,0:T(1,128)} %param.11) | copy-start | bytes 3076
  12.9 24.6 %copy-start.1 = (bf16[1,2048,256]{1,2,0:T(8,128)(2,1)}, bf16[1,2048,256]{1,2,0:T(8,128)(2,1)S(1)}, u32[]{:S(2)}) copy-start(bf16[1,2048,256]{1,2,0:T(8,128)(2,1)S(1)} %copy.135) | copy-start | bytes 3145732
  33.3 29.7 %all-to-all-start.2 = ((bf16[8,32,2048]{2,1,0:T(8,128)(2,1)}), bf16[8,32,2048]{2,1,0:T(8,128)(2,1)}, u32[]{:S(2)}, u32[]{:S(2)}) async-start(bf16[8,32,2048]{2,1,0:T(8,128)(2,1)} %bitcast.21), calls=%async_computation.2 | async-start | bytes 2097152 | tf_op jit(solution)/shard_map/all_to_all | solution.py:46
  40.4 29.7 %copy-start.24 = (bf16[1,64,32,32]{1,3,2,0:T(8,128)(2,1)S(1)}, bf16[1,64,32,32]{1,3,2,0:T(8,128)(2,1)}, u32[]{:S(2)}) copy-start(bf16[1,64,32,32]{1,3,2,0:T(8,128)(2,1)} %param.15) | copy-start | bytes 393220
  43.1 27.0 %copy-start.25 = (bf16[1,64,32,32]{1,3,2,0:T(8,128)(2,1)S(1)}, bf16[1,64,32,32]{1,3,2,0:T(8,128)(2,1)}, u32[]{:S(2)}) copy-start(bf16[1,64,32,32]{1,3,2,0:T(8,128)(2,1)} %param.17) | copy-start | bytes 393220
  63.0 21.0 %all-to-all-start = ((bf16[8,256,256]{2,0,1:T(8,128)(2,1)}), bf16[8,256,256]{2,0,1:T(8,128)(2,1)}, u32[]{:S(2)}, u32[]{:S(2)}) async-start(bf16[8,256,256]{2,0,1:T(8,128)(2,1)} %copy.92), calls=%async_computation | async-start | bytes 2097152 | tf_op jit(solution)/shard_map/all_to_all | solution.py:89
  84.0 27.3 %all-to-all-start.3 = ((bf16[8,32,2048]{2,1,0:T(8,128)(2,1)}), bf16[8,32,2048]{2,1,0:T(8,128)(2,1)S(1)}, u32[]{:S(2)}, u32[]{:S(2)}) async-start(bf16[8,32,2048]{2,1,0:T(8,128)(2,1)} %bitcast.247), calls=%async_computation.3 | async-start | bytes 2097152 | tf_op jit(solution)/shard_map/all_to_all | solution.py:50
  90.7 25.6 %copy-start.22 = (bf16[64,4,4,64]{3,2,1,0:T(4,128)(2,1)S(1)}, bf16[64,4,4,64]{3,2,1,0:T(4,128)(2,1)}, u32[]{:S(2)}) copy-start(bf16[64,4,4,64]{3,2,1,0:T(4,128)(2,1)} %get-tuple-element.35) | copy-start | bytes 393220
  111.3 26.8 %all-to-all-start.1 = ((bf16[128,16,256]{2,1,0:T(8,128)(2,1)}), bf16[128,16,256]{2,1,0:T(8,128)(2,1)}, u32[]{:S(2)}, u32[]{:S(2)}) async-start(bf16[128,16,256]{2,1,0:T(8,128)(2,1)} %copy.96), calls=%async_computation.1 | async-start | bytes 2097152 | tf_op jit(solution)/shard_map/all_to_all | solution.py:92
  141.2 30.0 %all-to-all-start.4 = ((bf16[8,32,2048]{2,1,0:T(8,128)(2,1)}), bf16[8,32,2048]{2,1,0:T(8,128)(2,1)}, u32[]{:S(2)}, u32[]{:S(2)}) async-start(bf16[8,32,2048]{2,1,0:T(8,128)(2,1)} %bitcast.250), calls=%async_computation.4 | async-start | bytes 2097152 | tf_op jit(solution)/shard_map/all_to_all | solution.py:66
  203.7 4.6 collective-permute-start
  229.9 29.7 %all-to-all-start.8 = ((bf16[8,32,2048]{2,1,0:T(8,128)(2,1)}), bf16[8,32,2048]{2,1,0:T(8,128)(2,1)}, u32[]{:S(2)}, u32[]{:S(2)}) async-start(bf16[8,32,2048]{2,1,0:T(8,128)(2,1)} %bitcast.251), calls=%async_computation.8 | async-start | bytes 2097152 | tf_op jit(solution)/shard_map/all_to_all | solution.py:46
  259.6 20.8 %all-to-all-start.6 = ((bf16[8,256,256]{2,0,1:T(8,128)(2,1)}), bf16[8,256,256]{2,0,1:T(8,128)(2,1)}, u32[]{:S(2)}, u32[]{:S(2)}) async-start(bf16[8,256,256]{2,0,1:T(8,128)(2,1)} %copy.106), calls=%async_computation.6 | async-start | bytes 2097152 | tf_op jit(solution)/shard_map/all_to_all | solution.py:89
  280.5 27.9 %all-to-all-start.9 = ((bf16[8,32,2048]{2,1,0:T(8,128)(2,1)}), bf16[8,32,2048]{2,1,0:T(8,128)(2,1)}, u32[]{:S(2)}, u32[]{:S(2)}) async-start(bf16[8,32,2048]{2,1,0:T(8,128)(2,1)} %bitcast.248), calls=%async_computation.9 | async-start | bytes 2097152 | tf_op jit(solution)/shard_map/all_to_all | solution.py:50
  308.4 31.3 %all-to-all-start.7 = ((bf16[128,16,256]{2,1,0:T(8,128)(2,1)}), bf16[128,16,256]{2,1,0:T(8,128)(2,1)}, u32[]{:S(2)}, u32[]{:S(2)}) async-start(bf16[128,16,256]{2,1,0:T(8,128)(2,1)} %copy.110), calls=%async_computation.7 | async-start | bytes 2097152 | tf_op jit(solution)/shard_map/all_to_all | solution.py:92
  400.1 3.6 collective-permute-start.1
  424.1 30.1 %all-to-all-start.14 = ((bf16[8,32,2048]{2,1,0:T(8,128)(2,1)}), bf16[8,32,2048]{2,1,0:T(8,128)(2,1)}, u32[]{:S(2)}, u32[]{:S(2)}) async-start(bf16[8,32,2048]{2,1,0:T(8,128)(2,1)} %bitcast.249), calls=%async_computation.14 | async-start | bytes 2097152 | tf_op jit(solution)/shard_map/all_to_all | solution.py:46
  454.1 20.8 %all-to-all-start.12 = ((bf16[8,256,256]{2,0,1:T(8,128)(2,1)}), bf16[8,256,256]{2,0,1:T(8,128)(2,1)}, u32[]{:S(2)}, u32[]{:S(2)}) async-start(bf16[8,256,256]{2,0,1:T(8,128)(2,1)} %copy.116), calls=%async_computation.12 | async-start | bytes 2097152 | tf_op jit(solution)/shard_map/all_to_all | solution.py:89
  474.9 28.1 %all-to-all-start.15 = ((bf16[8,32,2048]{2,1,0:T(8,128)(2,1)}), bf16[8,32,2048]{2,1,0:T(8,128)(2,1)}, u32[]{:S(2)}, u32[]{:S(2)}) async-start(bf16[8,32,2048]{2,1,0:T(8,128)(2,1)} %bitcast.246), calls=%async_computation.15 | async-start | bytes 2097152 | tf_op jit(solution)/shard_map/all_to_all | solution.py:50
  503.0 31.3 %all-to-all-start.13 = ((bf16[128,16,256]{2,1,0:T(8,128)(2,1)}), bf16[128,16,256]{2,1,0:T(8,128)(2,1)}, u32[]{:S(2)}, u32[]{:S(2)}) async-start(bf16[128,16,256]{2,1,0:T(8,128)(2,1)} %copy.120), calls=%async_computation.13 | async-start | bytes 2097152 | tf_op jit(solution)/shard_map/all_to_all | solution.py:92
  538.1 47.2 %all-to-all-start.16 = ((bf16[8,32,2048]{2,1,0:T(8,128)(2,1)}), bf16[8,32,2048]{2,1,0:T(8,128)(2,1)}, u32[]{:S(2)}, u32[]{:S(2)}) async-start(bf16[8,32,2048]{2,1,0:T(8,128)(2,1)} %bitcast.244), calls=%async_computation.16 | async-start | bytes 2097152 | tf_op jit(solution)/shard_map/all_to_all | solution.py:66
  542.3 127.1 %all-gather.4.cloned.1.call-start = ((), (), s32[]{:S(2)}) async-start(), calls=%async_computation.18 | async-start | bytes 1114112 | tf_op jit(solution)/shard_map/all_gather | solution.py:167
  587.9 44.8 %all-to-all-start.17 = ((bf16[8,32,2048]{2,1,0:T(8,128)(2,1)}), bf16[8,32,2048]{2,1,0:T(8,128)(2,1)}, u32[]{:S(2)}, u32[]{:S(2)}) async-start(bf16[8,32,2048]{2,1,0:T(8,128)(2,1)} %bitcast.245), calls=%async_computation.17 | async-start | bytes 2097152 | tf_op jit(solution)/shard_map/all_to_all | solution.py:70
  593.7 89.2 %all-gather.6.cloned.1.call-start = ((), (), s32[]{:S(2)}) async-start(), calls=%async_computation.19 | async-start | bytes 1114112 | tf_op jit(solution)/shard_map/all_gather | solution.py:167
  632.7 99.7 %all-gather.8.cloned.1.call-start = ((), (), s32[]{:S(2)}) async-start(), calls=%async_computation.20 | async-start | bytes 1114112 | tf_op jit(solution)/shard_map/all_gather | solution.py:167
  636.7 30.1 %copy-start.27 = (s32[2,256]{1,0:T(2,128)S(1)}, s32[2,256]{1,0:T(2,128)}, u32[]{:S(2)}) copy-start(s32[2,256]{1,0:T(2,128)} %param.19) | copy-start | bytes 6148
  669.4 16.4 %copy-start.11 = (bf16[2048,256]{0,1:T(8,128)(2,1)S(1)}, bf16[2048,256]{0,1:T(8,128)(2,1)}, u32[]{:S(2)}) copy-start(bf16[2048,256]{0,1:T(8,128)(2,1)} %copy-done.10) | copy-start | bytes 3145732
  669.4 16.4 %copy-start.12 = (bf16[2048,256]{0,1:T(8,128)(2,1)S(1)}, bf16[2048,256]{0,1:T(8,128)(2,1)}, u32[]{:S(2)}) copy-start(bf16[2048,256]{0,1:T(8,128)(2,1)} %fusion.7) | copy-start | bytes 3145732
  687.4 44.9 %copy-start.17 = (bf16[1,2048,256]{2,1,0:T(8,128)(2,1)S(1)}, bf16[1,2048,256]{2,1,0:T(8,128)(2,1)}, u32[]{:S(2)}) copy-start(bf16[1,2048,256]{2,1,0:T(8,128)(2,1)} %param.18) | copy-start | bytes 3145732
  687.4 44.9 %copy-start.23 = (f32[256,256]{0,1:T(8,128)S(1)}, f32[256,256]{0,1:T(8,128)}, u32[]{:S(2)}) copy-start(f32[256,256]{0,1:T(8,128)} %fusion.34) | copy-start | bytes 786436
  (16 other events, 39.9 us)
Sparse Core Ops, SparseCore 0:
  585.4 47.9 all-gather.3
  635.8 47.0 all-gather.5
  685.3 47.0 all-gather.7
where the time goes:
time: 1100 us; the launch traced here: 1090 us
  blocking collectives  578 us (53%)
  waiting for transfers between devices  219 us (20%)
  local copies, waits for them, and re-layouts  132 us (12%)
  starting transfers between devices  78.2 us (7%)
  matrix products  38.8 us (4%)
  other arithmetic  32.9 us (3%)
  between operations  14.8 us (1%)
    psum x1, blocking collectives, body(): lax.psum((exp_sums, target_part), ('seq', 'tensor'))  352 us
    all_gather x3, blocking collectives, body(): wide_rows = lax.all_gather(scored, 'tensor', axis=1, tiled=True)  94.1 us
    div x9, local copies, waits for them, and re-layouts, body(): jax.nn.sigmoid(gate_pre.astype(jnp.float32))  70.5 us
    all_to_all x3, waiting for transfers between devices, gate_channels(): lax.all_to_all(first_mix, 'tensor', split_axis=0, concat_axis=0, tiled=True)  60.5 us
    all_to_all x2, blocking collectives, out_channels(): lax.all_to_all(second_mix.reshape(groups, c_one * k_dev, count_here), 'te...  55.5 us
    all_to_all x3, waiting for transfers between devices, gate_channels(): lax.all_to_all(second_mix.reshape(groups, c_one * k_dev, count_here), 'te...  53.8 us
    all_gather x3, waiting for transfers between devices, body(): lax.all_gather(wide_rows, 'seq', axis=0, tiled=True)  52.1 us
    psum x3, blocking collectives, body(): square_total = lax.psum(square_part, 'tensor')  48.4 us
  transfers between devices with their start and end apart: 20, of which 13 were waited for; matrix products, arithmetic and copies ran while one was open for 15% of the time, Pallas kernels for 0%

commit v1 on v0

--- a/solution.py
+++ b/solution.py
@@ -172,7 +172,7 @@
         vocab_ids = jnp.arange(vocab_dev, dtype=jnp.int32)[None, :] + vocab_offset
         is_target = vocab_ids == labels[:, None]
         target_part = jnp.sum(jnp.where(is_target, logits, 0.0), axis=1)
-        exp_total, target_logit = lax.psum((exp_sums, target_part), ("seq", "tensor"))
+        exp_total, target_logit = lax.psum(lax.psum((exp_sums, target_part), "seq"), "tensor")
         result, aux_loss = (result, jnp.log(exp_total) - target_logit)
         if step_index < micro_count:
             first_outputs.append(result)

time: 1100 us -> 809 us (0.74)
  blocking collectives: 578 us -> 282 us
    psum x1 -> x2, blocking collectives: 352 us -> 56.4 us  [the longest x1 38.7 us: body(): lax.psum((exp_sums, target_part), 'seq')]
  transfers between devices with their start and end apart: 20 -> 20, of which waited for: 13 -> 13; matrix products, arithmetic and copies ran while one was open for 15% -> 20% of each run, Pallas kernels for 0% -> 0%
where the time goes in v1:
time: 809 us; the launch traced here: 798 us
  blocking collectives  282 us (35%)
  waiting for transfers between devices  220 us (27%)
  local copies, waits for them, and re-layouts  132 us (16%)
  starting transfers between devices  78.2 us (10%)
  matrix products  38.8 us (5%)
  other arithmetic  32.8 us (4%)
  between operations  14.8 us (2%)
    all_gather x3, blocking collectives, body(): wide_rows = lax.all_gather(scored, 'tensor', axis=1, tiled=True)  93.8 us
    div x9, local copies, waits for them, and re-layouts, body(): jax.nn.sigmoid(gate_pre.astype(jnp.float32))  70.5 us
    all_to_all x3, waiting for transfers between devices, gate_channels(): lax.all_to_all(first_mix, 'tensor', split_axis=0, concat_axis=0, tiled=True)  60.6 us
    all_to_all x2, blocking collectives, out_channels(): lax.all_to_all(second_mix.reshape(groups, c_one * k_dev, count_here), 'te...  55.5 us
    all_to_all x3, waiting for transfers between devices, gate_channels(): lax.all_to_all(second_mix.reshape(groups, c_one * k_dev, count_here), 'te...  53.8 us
    all_gather x3, waiting for transfers between devices, body(): lax.all_gather(wide_rows, 'seq', axis=0, tiled=True)  52.5 us
    psum x3, blocking collectives, body(): square_total = lax.psum(square_part, 'tensor')  48.4 us
    psum x1, blocking collectives, body(): lax.psum((exp_sums, target_part), 'seq')  38.7 us
  transfers between devices with their start and end apart: 20, of which 13 were waited for; matrix products, arithmetic and copies ran while one was open for 20% of the time, Pallas kernels for 0%

profile of v1, /device:TPU:0, one launch (start us, length us, event | category | flops | bytes accessed | tf_op | source)
XLA Modules:
  0.0 797.9 jit_solution(1166024801991567434)
XLA Ops:
  13.2 18.5 %psum.105 = f32[2048]{0:T(1024)S(1)} all-reduce(f32[2048]{0:T(1024)S(1)} %fusion.18), channel_id=1, replica_groups=mesh['section'=2,'seq'=16,'tensor'=8] {'tensor'}, use_global_device_ids=true, to_apply=%region_1.2 | all-reduce | flops 2048 | bytes 16384 | tf_op jit(solution)/shard_map/psum | solution.py:152
  43.1 19.9 %all-to-all-done.2 = bf16[8,32,2048]{2,1,0:T(8,128)(2,1)} async-done(((bf16[8,32,2048]{2,1,0:T(8,128)(2,1)}), bf16[8,32,2048]{2,1,0:T(8,128)(2,1)}, u32[]{:S(2)}, u32[]{:S(2)}) %all-to-all-start.2) | async-done | bytes 1048608 | tf_op jit(solution)/shard_map/all_to_all | solution.py:46
  63.0 7.1 all-to-all-start
  93.4 17.9 %all-to-all-done.3 = bf16[8,32,2048]{2,1,0:T(8,128)(2,1)S(1)} async-done(((bf16[8,32,2048]{2,1,0:T(8,128)(2,1)}), bf16[8,32,2048]{2,1,0:T(8,128)(2,1)S(1)}, u32[]{:S(2)}, u32[]{:S(2)}) %all-to-all-start.3) | async-done | bytes 1048608 | tf_op jit(solution)/shard_map/all_to_all | solution.py:50
  117.2 9.1 %reshape.474 = f32[8,16,16,256]{2,1,0,3:T(8,128)} reshape(f32[2048,4,8,8]{0,3,2,1:T(8,128)S(1)} %copy.99) | data formatting | bytes 4194304 | tf_op jit(solution)/shard_map/div | solution.py:158
  126.2 11.8 %copy.100 = f32[8,16,16,256]{3,2,0,1:T(8,128)S(1)} copy(f32[8,16,16,256]{2,1,0,3:T(8,128)} %reshape.474) | data formatting | bytes 4194304 | tf_op jit(solution)/shard_map/div | solution.py:158
  148.3 22.9 %all-to-all-done.4 = bf16[8,32,2048]{2,1,0:T(8,128)(2,1)} async-done(((bf16[8,32,2048]{2,1,0:T(8,128)(2,1)}), bf16[8,32,2048]{2,1,0:T(8,128)(2,1)}, u32[]{:S(2)}, u32[]{:S(2)}) %all-to-all-start.4) | async-done | bytes 1048608 | tf_op jit(solution)/shard_map/all_to_all | solution.py:66
  172.8 28.1 %all_to_all.141 = bf16[8,32,2048]{2,1,0:T(8,128)(2,1)S(1)} all-to-all(bf16[8,32,2048]{2,1,0:T(8,128)(2,1)S(1)} %bitcast.255), channel_id=1, replica_groups=mesh['section'=2,'seq'=16,'tensor'=8] {'tensor'}, dimensions={0} | all-to-all | bytes 2097152 | tf_op jit(solution)/shard_map/all_to_all | solution.py:70
  210.9 14.9 %psum.106 = f32[2048]{0:T(1024)S(1)} all-reduce(f32[2048]{0:T(1024)S(1)} %get-tuple-element.28), channel_id=1, replica_groups=mesh['section'=2,'seq'=16,'tensor'=8] {'tensor'}, use_global_device_ids=true, to_apply=%region_3.4 | all-reduce | flops 2048 | bytes 16384 | tf_op jit(solution)/shard_map/psum | solution.py:152
  239.4 20.2 %all-to-all-done.8 = bf16[8,32,2048]{2,1,0:T(8,128)(2,1)} async-done(((bf16[8,32,2048]{2,1,0:T(8,128)(2,1)}), bf16[8,32,2048]{2,1,0:T(8,128)(2,1)}, u32[]{:S(2)}, u32[]{:S(2)}) %all-to-all-start.8) | async-done | bytes 1048608 | tf_op jit(solution)/shard_map/all_to_all | solution.py:46
  259.6 7.0 all-to-all-start.6
  269.2 11.2 %all-to-all-done.6 = bf16[8,256,256]{2,0,1:T(8,128)(2,1)} async-done(((bf16[8,256,256]{2,0,1:T(8,128)(2,1)}), bf16[8,256,256]{2,0,1:T(8,128)(2,1)}, u32[]{:S(2)}, u32[]{:S(2)}) %all-to-all-start.6) | async-done | bytes 1048608 | tf_op jit(solution)/shard_map/all_to_all | solution.py:89
  290.4 17.9 %all-to-all-done.9 = bf16[8,32,2048]{2,1,0:T(8,128)(2,1)} async-done(((bf16[8,32,2048]{2,1,0:T(8,128)(2,1)}), bf16[8,32,2048]{2,1,0:T(8,128)(2,1)}, u32[]{:S(2)}, u32[]{:S(2)}) %all-to-all-start.9) | async-done | bytes 1048608 | tf_op jit(solution)/shard_map/all_to_all | solution.py:50
  316.2 10.4 %reshape.479 = f32[8,16,16,256]{2,1,0,3:T(8,128)} reshape(f32[2048,4,8,8]{0,3,2,1:T(8,128)} %copy.111) | data formatting | bytes 4194304 | tf_op jit(solution)/shard_map/div | solution.py:158
  326.7 12.9 %copy.112 = f32[8,16,16,256]{3,2,0,1:T(8,128)} copy(f32[8,16,16,256]{2,1,0,3:T(8,128)} %reshape.479) | data formatting | bytes 4194304 | tf_op jit(solution)/shard_map/div | solution.py:158
  342.3 28.1 %all_to_all.142 = bf16[8,32,2048]{2,1,0:T(8,128)(2,1)S(1)} all-to-all(bf16[8,32,2048]{2,1,0:T(8,128)(2,1)S(1)} %bitcast.258), channel_id=1, replica_groups=mesh['section'=2,'seq'=16,'tensor'=8] {'tensor'}, dimensions={0} | all-to-all | bytes 2097152 | tf_op jit(solution)/shard_map/all_to_all | solution.py:66
  370.9 27.4 %all_to_all.143 = bf16[8,32,2048]{2,1,0:T(8,128)(2,1)S(1)} all-to-all(bf16[8,32,2048]{2,1,0:T(8,128)(2,1)S(1)} %bitcast.260), channel_id=1, replica_groups=mesh['section'=2,'seq'=16,'tensor'=8] {'tensor'}, dimensions={0} | all-to-all | bytes 2097152 | tf_op jit(solution)/shard_map/all_to_all | solution.py:70
  405.0 15.0 %psum.107 = f32[2048]{0:T(1024)S(1)} all-reduce(f32[2048]{0:T(1024)S(1)} %get-tuple-element.26), channel_id=1, replica_groups=mesh['section'=2,'seq'=16,'tensor'=8] {'tensor'}, use_global_device_ids=true, to_apply=%region_5.6 | all-reduce | flops 2048 | bytes 16384 | tf_op jit(solution)/shard_map/psum | solution.py:152
  433.5 20.5 %all-to-all-done.14 = bf16[8,32,2048]{2,1,0:T(8,128)(2,1)} async-done(((bf16[8,32,2048]{2,1,0:T(8,128)(2,1)}), bf16[8,32,2048]{2,1,0:T(8,128)(2,1)}, u32[]{:S(2)}, u32[]{:S(2)}) %all-to-all-start.14) | async-done | bytes 1048608 | tf_op jit(solution)/shard_map/all_to_all | solution.py:46
  454.0 6.9 all-to-all-start.12
  463.6 11.3 %all-to-all-done.12 = bf16[8,256,256]{2,0,1:T(8,128)(2,1)} async-done(((bf16[8,256,256]{2,0,1:T(8,128)(2,1)}), bf16[8,256,256]{2,0,1:T(8,128)(2,1)}, u32[]{:S(2)}, u32[]{:S(2)}) %all-to-all-start.12) | async-done | bytes 1048608 | tf_op jit(solution)/shard_map/all_to_all | solution.py:89
  484.8 18.1 %all-to-all-done.15 = bf16[8,32,2048]{2,1,0:T(8,128)(2,1)} async-done(((bf16[8,32,2048]{2,1,0:T(8,128)(2,1)}), bf16[8,32,2048]{2,1,0:T(8,128)(2,1)}, u32[]{:S(2)}, u32[]{:S(2)}) %all-to-all-start.15) | async-done | bytes 1048608 | tf_op jit(solution)/shard_map/all_to_all | solution.py:50
  510.9 10.4 %reshape.483 = f32[8,16,16,256]{2,1,0,3:T(8,128)} reshape(f32[2048,4,8,8]{0,3,2,1:T(8,128)} %copy.121) | data formatting | bytes 4194304 | tf_op jit(solution)/shard_map/div | solution.py:158
  521.3 12.9 %copy.122 = f32[8,16,16,256]{3,2,0,1:T(8,128)} copy(f32[8,16,16,256]{2,1,0,3:T(8,128)} %reshape.483) | data formatting | bytes 4194304 | tf_op jit(solution)/shard_map/div | solution.py:158
  545.1 6.3 slice.28
  552.8 32.3 %all_gather.18 = bf16[16,2048]{1,0:T(8,128)(2,1)} all-gather(bf16[16,256]{1,0:T(8,128)(2,1)S(1)} %reshape.465), channel_id=1, replica_groups=mesh['section'=2,'seq'=16,'tensor'=8] {'tensor'}, dimensions={1}, use_global_device_ids=true | all-gather | bytes 73728 | tf_op jit(solution)/shard_map/all_gather | solution.py:165
  597.3 34.9 %all_gather.20 = bf16[16,2048]{1,0:T(8,128)(2,1)} all-gather(bf16[16,256]{1,0:T(8,128)(2,1)S(1)} %reshape.467), channel_id=1, replica_groups=mesh['section'=2,'seq'=16,'tensor'=8] {'tensor'}, dimensions={1}, use_global_device_ids=true | all-gather | bytes 73728 | tf_op jit(solution)/shard_map/all_gather | solution.py:165
  639.8 26.5 %all_gather.22 = bf16[16,2048]{1,0:T(8,128)(2,1)} all-gather(bf16[16,256]{1,0:T(8,128)(2,1)S(1)} %reshape.469), channel_id=1, replica_groups=mesh['section'=2,'seq'=16,'tensor'=8] {'tensor'}, dimensions={1}, use_global_device_ids=true | all-gather | bytes 73728 | tf_op jit(solution)/shard_map/all_gather | solution.py:165
  671.2 11.6 %all-gather.6.cloned.1.call-done = bf16[256,2048]{1,0:T(8,128)(2,1)} async-done(((bf16[16,2048]{1,0:T(8,128)(2,1)}), bf16[256,2048]{1,0:T(8,128)(2,1)}) %all-gather.6.cloned.1.call-update) | async-done | bytes 1048592 | tf_op jit(solution)/shard_map/all_gather | solution.py:167
  691.4 40.9 %all-gather.8.cloned.1.call-done = bf16[256,2048]{1,0:T(8,128)(2,1)} async-done(((bf16[16,2048]{1,0:T(8,128)(2,1)}), bf16[256,2048]{1,0:T(8,128)(2,1)}) %all-gather.8.cloned.1.call-update) | async-done | bytes 1048592 | tf_op jit(solution)/shard_map/all_gather | solution.py:167
  734.1 38.7 %all-reduce = (f32[256]{0:T(256)S(1)}, f32[256]{0:T(256)S(1)}, f32[256]{0:T(256)S(1)}, f32[256]{0:T(256)S(1)}, f32[256]{0:T(256)S(1)}, /*index=5*/f32[256]{0:T(256)S(1)}) all-reduce(f32[256]{0:T(256)S(1)} %get-tuple-element.36, f32[256]{0:T(256)S(1)} %get-tuple-element.37, ...), channel_id=1, replica_groups=mesh['section'=2,'seq'=16,'tensor'=8] {'seq'}, use_global_device_ids=true, to_apply=%region_16.17 | all-reduce | flops 1536 | bytes 12288 | tf_op jit(solution)/shard_map/psum | solution.py:175
  772.8 17.7 %all-reduce.1 = (f32[256]{0:T(256)S(1)}, f32[256]{0:T(256)S(1)}, f32[256]{0:T(256)S(1)}, f32[256]{0:T(256)S(1)}, f32[256]{0:T(256)S(1)}, /*index=5*/f32[256]{0:T(256)S(1)}) all-reduce(f32[256]{0:T(256)S(1)} %get-tuple-element.14, f32[256]{0:T(256)S(1)} %get-tuple-element.15, ...), channel_id=1, replica_groups=mesh['section'=2,'seq'=16,'tensor'=8] {'tensor'}, use_global_device_ids=true, to_apply=%region_17.18 | all-reduce | flops 1536 | bytes 12288 | tf_op jit(solution)/shard_map/psum | solution.py:175
  (185 shorter events, 194.0 us)
Async XLA Ops:
  7.2 31.8 %copy-start = (bf16[1,8,256,256]{3,2,1,0:T(8,128)(2,1)S(1)}, bf16[1,8,256,256]{3,2,1,0:T(8,128)(2,1)}, u32[]{:S(2)}) copy-start(bf16[1,8,256,256]{3,2,1,0:T(8,128)(2,1)} %param.12) | copy-start | bytes 3145732
  9.6 22.2 %copy-start.19 = (bf16[256,256]{1,0:T(8,128)(2,1)}, bf16[256,256]{1,0:T(8,128)(2,1)S(1)}, u32[]{:S(2)}) copy-start(bf16[256,256]{1,0:T(8,128)(2,1)S(1)} %mul.236) | copy-start | bytes 393220
  12.3 19.5 %copy-start.26 = (f32[1,256]{1,0:T(1,128)S(1)}, f32[1,256]{1,0:T(1,128)}, u32[]{:S(2)}) copy-start(f32[1,256]{1,0:T(1,128)} %param.11) | copy-start | bytes 3076
  12.9 24.6 %copy-start.1 = (bf16[1,2048,256]{1,2,0:T(8,128)(2,1)}, bf16[1,2048,256]{1,2,0:T(8,128)(2,1)S(1)}, u32[]{:S(2)}) copy-start(bf16[1,2048,256]{1,2,0:T(8,128)(2,1)S(1)} %copy.135) | copy-start | bytes 3145732
  33.3 29.7 %all-to-all-start.2 = ((bf16[8,32,2048]{2,1,0:T(8,128)(2,1)}), bf16[8,32,2048]{2,1,0:T(8,128)(2,1)}, u32[]{:S(2)}, u32[]{:S(2)}) async-start(bf16[8,32,2048]{2,1,0:T(8,128)(2,1)} %bitcast.21), calls=%async_computation.2 | async-start | bytes 2097152 | tf_op jit(solution)/shard_map/all_to_all | solution.py:46
  40.4 29.7 %copy-start.24 = (bf16[1,64,32,32]{1,3,2,0:T(8,128)(2,1)S(1)}, bf16[1,64,32,32]{1,3,2,0:T(8,128)(2,1)}, u32[]{:S(2)}) copy-start(bf16[1,64,32,32]{1,3,2,0:T(8,128)(2,1)} %param.15) | copy-start | bytes 393220
  43.1 27.0 %copy-start.25 = (bf16[1,64,32,32]{1,3,2,0:T(8,128)(2,1)S(1)}, bf16[1,64,32,32]{1,3,2,0:T(8,128)(2,1)}, u32[]{:S(2)}) copy-start(bf16[1,64,32,32]{1,3,2,0:T(8,128)(2,1)} %param.17) | copy-start | bytes 393220
  63.0 20.9 %all-to-all-start = ((bf16[8,256,256]{2,0,1:T(8,128)(2,1)}), bf16[8,256,256]{2,0,1:T(8,128)(2,1)}, u32[]{:S(2)}, u32[]{:S(2)}) async-start(bf16[8,256,256]{2,0,1:T(8,128)(2,1)} %copy.92), calls=%async_computation | async-start | bytes 2097152 | tf_op jit(solution)/shard_map/all_to_all | solution.py:89
  84.0 27.3 %all-to-all-start.3 = ((bf16[8,32,2048]{2,1,0:T(8,128)(2,1)}), bf16[8,32,2048]{2,1,0:T(8,128)(2,1)S(1)}, u32[]{:S(2)}, u32[]{:S(2)}) async-start(bf16[8,32,2048]{2,1,0:T(8,128)(2,1)} %bitcast.247), calls=%async_computation.3 | async-start | bytes 2097152 | tf_op jit(solution)/shard_map/all_to_all | solution.py:50
  90.7 25.6 %copy-start.22 = (bf16[64,4,4,64]{3,2,1,0:T(4,128)(2,1)S(1)}, bf16[64,4,4,64]{3,2,1,0:T(4,128)(2,1)}, u32[]{:S(2)}) copy-start(bf16[64,4,4,64]{3,2,1,0:T(4,128)(2,1)} %get-tuple-element.41) | copy-start | bytes 393220
  111.2 26.8 %all-to-all-start.1 = ((bf16[128,16,256]{2,1,0:T(8,128)(2,1)}), bf16[128,16,256]{2,1,0:T(8,128)(2,1)}, u32[]{:S(2)}, u32[]{:S(2)}) async-start(bf16[128,16,256]{2,1,0:T(8,128)(2,1)} %copy.96), calls=%async_computation.1 | async-start | bytes 2097152 | tf_op jit(solution)/shard_map/all_to_all | solution.py:92
  141.1 30.0 %all-to-all-start.4 = ((bf16[8,32,2048]{2,1,0:T(8,128)(2,1)}), bf16[8,32,2048]{2,1,0:T(8,128)(2,1)}, u32[]{:S(2)}, u32[]{:S(2)}) async-start(bf16[8,32,2048]{2,1,0:T(8,128)(2,1)} %bitcast.250), calls=%async_computation.4 | async-start | bytes 2097152 | tf_op jit(solution)/shard_map/all_to_all | solution.py:66
  203.7 4.5 collective-permute-start
  229.8 29.8 %all-to-all-start.8 = ((bf16[8,32,2048]{2,1,0:T(8,128)(2,1)}), bf16[8,32,2048]{2,1,0:T(8,128)(2,1)}, u32[]{:S(2)}, u32[]{:S(2)}) async-start(bf16[8,32,2048]{2,1,0:T(8,128)(2,1)} %bitcast.251), calls=%async_computation.8 | async-start | bytes 2097152 | tf_op jit(solution)/shard_map/all_to_all | solution.py:46
  259.6 20.8 %all-to-all-start.6 = ((bf16[8,256,256]{2,0,1:T(8,128)(2,1)}), bf16[8,256,256]{2,0,1:T(8,128)(2,1)}, u32[]{:S(2)}, u32[]{:S(2)}) async-start(bf16[8,256,256]{2,0,1:T(8,128)(2,1)} %copy.106), calls=%async_computation.6 | async-start | bytes 2097152 | tf_op jit(solution)/shard_map/all_to_all | solution.py:89
  280.4 27.9 %all-to-all-start.9 = ((bf16[8,32,2048]{2,1,0:T(8,128)(2,1)}), bf16[8,32,2048]{2,1,0:T(8,128)(2,1)}, u32[]{:S(2)}, u32[]{:S(2)}) async-start(bf16[8,32,2048]{2,1,0:T(8,128)(2,1)} %bitcast.248), calls=%async_computation.9 | async-start | bytes 2097152 | tf_op jit(solution)/shard_map/all_to_all | solution.py:50
  308.3 31.3 %all-to-all-start.7 = ((bf16[128,16,256]{2,1,0:T(8,128)(2,1)}), bf16[128,16,256]{2,1,0:T(8,128)(2,1)}, u32[]{:S(2)}, u32[]{:S(2)}) async-start(bf16[128,16,256]{2,1,0:T(8,128)(2,1)} %copy.110), calls=%async_computation.7 | async-start | bytes 2097152 | tf_op jit(solution)/shard_map/all_to_all | solution.py:92
  400.0 3.6 collective-permute-start.1
  424.0 30.1 %all-to-all-start.14 = ((bf16[8,32,2048]{2,1,0:T(8,128)(2,1)}), bf16[8,32,2048]{2,1,0:T(8,128)(2,1)}, u32[]{:S(2)}, u32[]{:S(2)}) async-start(bf16[8,32,2048]{2,1,0:T(8,128)(2,1)} %bitcast.249), calls=%async_computation.14 | async-start | bytes 2097152 | tf_op jit(solution)/shard_map/all_to_all | solution.py:46
  454.0 20.8 %all-to-all-start.12 = ((bf16[8,256,256]{2,0,1:T(8,128)(2,1)}), bf16[8,256,256]{2,0,1:T(8,128)(2,1)}, u32[]{:S(2)}, u32[]{:S(2)}) async-start(bf16[8,256,256]{2,0,1:T(8,128)(2,1)} %copy.116), calls=%async_computation.12 | async-start | bytes 2097152 | tf_op jit(solution)/shard_map/all_to_all | solution.py:89
  474.8 28.1 %all-to-all-start.15 = ((bf16[8,32,2048]{2,1,0:T(8,128)(2,1)}), bf16[8,32,2048]{2,1,0:T(8,128)(2,1)}, u32[]{:S(2)}, u32[]{:S(2)}) async-start(bf16[8,32,2048]{2,1,0:T(8,128)(2,1)} %bitcast.246), calls=%async_computation.15 | async-start | bytes 2097152 | tf_op jit(solution)/shard_map/all_to_all | solution.py:50
  502.9 31.3 %all-to-all-start.13 = ((bf16[128,16,256]{2,1,0:T(8,128)(2,1)}), bf16[128,16,256]{2,1,0:T(8,128)(2,1)}, u32[]{:S(2)}, u32[]{:S(2)}) async-start(bf16[128,16,256]{2,1,0:T(8,128)(2,1)} %copy.120), calls=%async_computation.13 | async-start | bytes 2097152 | tf_op jit(solution)/shard_map/all_to_all | solution.py:92
  537.9 47.3 %all-to-all-start.16 = ((bf16[8,32,2048]{2,1,0:T(8,128)(2,1)}), bf16[8,32,2048]{2,1,0:T(8,128)(2,1)}, u32[]{:S(2)}, u32[]{:S(2)}) async-start(bf16[8,32,2048]{2,1,0:T(8,128)(2,1)} %bitcast.244), calls=%async_computation.16 | async-start | bytes 2097152 | tf_op jit(solution)/shard_map/all_to_all | solution.py:66
  542.2 126.7 %all-gather.4.cloned.1.call-start = ((), (), s32[]{:S(2)}) async-start(), calls=%async_computation.18 | async-start | bytes 1114112 | tf_op jit(solution)/shard_map/all_gather | solution.py:167
  587.9 44.4 %all-to-all-start.17 = ((bf16[8,32,2048]{2,1,0:T(8,128)(2,1)}), bf16[8,32,2048]{2,1,0:T(8,128)(2,1)}, u32[]{:S(2)}, u32[]{:S(2)}) async-start(bf16[8,32,2048]{2,1,0:T(8,128)(2,1)} %bitcast.245), calls=%async_computation.17 | async-start | bytes 2097152 | tf_op jit(solution)/shard_map/all_to_all | solution.py:70
  593.6 89.2 %all-gather.6.cloned.1.call-start = ((), (), s32[]{:S(2)}) async-start(), calls=%async_computation.19 | async-start | bytes 1114112 | tf_op jit(solution)/shard_map/all_gather | solution.py:167
  632.2 100.1 %all-gather.8.cloned.1.call-start = ((), (), s32[]{:S(2)}) async-start(), calls=%async_computation.20 | async-start | bytes 1114112 | tf_op jit(solution)/shard_map/all_gather | solution.py:167
  636.2 30.1 %copy-start.27 = (s32[2,256]{1,0:T(2,128)S(1)}, s32[2,256]{1,0:T(2,128)}, u32[]{:S(2)}) copy-start(s32[2,256]{1,0:T(2,128)} %param.19) | copy-start | bytes 6148
  668.9 16.8 %copy-start.11 = (bf16[2048,256]{0,1:T(8,128)(2,1)S(1)}, bf16[2048,256]{0,1:T(8,128)(2,1)}, u32[]{:S(2)}) copy-start(bf16[2048,256]{0,1:T(8,128)(2,1)} %copy-done.10) | copy-start | bytes 3145732
  668.9 16.8 %copy-start.12 = (bf16[2048,256]{0,1:T(8,128)(2,1)S(1)}, bf16[2048,256]{0,1:T(8,128)(2,1)}, u32[]{:S(2)}) copy-start(bf16[2048,256]{0,1:T(8,128)(2,1)} %fusion.7) | copy-start | bytes 3145732
  687.4 44.9 %copy-start.17 = (bf16[1,2048,256]{2,1,0:T(8,128)(2,1)S(1)}, bf16[1,2048,256]{2,1,0:T(8,128)(2,1)}, u32[]{:S(2)}) copy-start(bf16[1,2048,256]{2,1,0:T(8,128)(2,1)} %param.18) | copy-start | bytes 3145732
  687.4 44.9 %copy-start.23 = (f32[256,256]{0,1:T(8,128)S(1)}, f32[256,256]{0,1:T(8,128)}, u32[]{:S(2)}) copy-start(f32[256,256]{0,1:T(8,128)} %fusion.34) | copy-start | bytes 786436
  (16 other events, 39.9 us)
Sparse Core Ops, SparseCore 0:
  585.3 47.9 all-gather.3
  635.8 47.0 all-gather.5
  685.2 47.0 all-gather.7
